TPU v7x, 32 devices: a whole 2x2x4 slice. The times are simulated.
32 devices in a mesh: row: 4 (over x, core), col: 8 (over z, y).
Axes of the slice: x: 2, y: 2, z: 4, core: 2. Of those that a mesh axis runs over, the one named last changes fastest.
Arguments:
- trailing: float32 [4096, 4096], P('row', 'col'), may hold values from -6 to 6
- panel_left: float32 [4096, 384], P(('row', 'col')), may hold values from -0.3125 to 0.3125
- panel_right: float32 [8, 1024, 384], P('row', 'col'), may hold values from -1 to 1
- panel_solved: float32 [1024, 1024], P('row', 'col'), may hold values from -1.75 to 1.75
- right_sides: float32 [4096, 1024], P('row', 'col'), may hold values from -6 to 6
- tile_ranks: int32 [8], replicated, may hold values from 64 to 384, as said below
- tile_order: int32 [8], replicated, may hold values from 0 to 7, each once
Outputs:
- trail_new: float32 [4096, 4096], P('row', 'col')
- rhs_new: float32 [4096, 1024], P('row', 'col')
Inputs may be any that keep to these rules, and one draw needn't show every extreme that they name: `tile_ranks`: every rank is a multiple of 64; both 64 and 384 occur in every draw. `tile_order`: each tile appears in exactly one slot.
All inputs are finite; a program needn't handle non-finite values.
Results may differ from a plain program's by a relative error of at most 0.00008.
Values sent between devices are 32-bit elements; how exact they have to be, the bound alone decides.
A program may use at most 64 MiB of HBM per device.

v0:
```python
import functools

import jax
import jax.numpy as jnp
from jax import lax
from jax.experimental import pallas as pl
from jax.experimental.pallas import tpu as pltpu
from jax.sharding import PartitionSpec as P

MESH = pl.DeviceIdType.MESH
ACROSS = 2
CORES = 2


def sides(z, length, d, body):
    for side in range(2):
        src = z - d if side == 0 else z + d
        ok = src >= 0 if side == 0 else (src < length) & (d > 0)
        pl.when(ok & (d >= 0))(functools.partial(body, src, side))


def find(order, value):
    place = jnp.int32(0)
    for i in range(order.shape[0]):
        place = jnp.where(order[i] == value, jnp.int32(i), place)
    return place


def gather_kernel(n_row, n_col, slots, order, left, right, solved, rows_l, both_out, tile,
                  rows_r, rows_w, first_out, first_in, chip, far_in, own_sem, rsem, zsem, ysem, fsem, frsem, xsem, xrsem, tsem, trsem, wsem, wrsem):
    length = n_col // ACROSS
    half = length // slots
    teams = n_row // CORES
    part = tile.shape[1] // CORES
    late = slots + 1
    row, col = lax.axis_index("row"), lax.axis_index("col")
    z, y = col // ACROSS, col % ACROSS
    team, core = row // CORES, row % CORES
    pair = team * CORES + (1 - core)
    mate = z * ACROSS + (1 - y)

    barrier = pltpu.get_barrier_semaphore()

    def greet(r, c):
        pl.semaphore_signal(barrier, inc=1, device_id=(r, c), device_id_type=MESH)

    @pl.when(z > 0)
    def _():
        greet(row, col - ACROSS)

    @pl.when(z < length - 1)
    def _():
        greet(row, col + ACROSS)

    greet(row, mate)
    for k in range(1, n_row):
        greet(lax.rem(row + k, n_row), col)

    cut = left.shape[0] // 2

    def piece(p, c):
        if p == 0:
            return rows_l.at[c, pl.ds(0, cut)]
        if p == late:
            return rows_l.at[c, pl.ds(cut, cut)]
        return rows_r.at[p - 1, c]

    own = [pltpu.make_async_copy(left, rows_l.at[col], own_sem.at[0])]
    for s in range(slots):
        own.append(pltpu.make_async_copy(right.at[s], piece(s + 1, col), own_sem.at[s + 1]))
    own.append(pltpu.make_async_copy(solved, rows_w.at[row], own_sem.at[slots + 1]))
    for copy in own:
        copy.start()
    for copy in own:
        copy.wait()
    pl.semaphore_wait(barrier, (z > 0).astype(jnp.int32) + (z < length - 1).astype(jnp.int32) + n_row)

    def z_copy(p, src, way, across=None):
        c = src * ACROSS + (y if across is None else across)
        lane = p if across is None else late + 1
        to = col + (ACROSS if way == 0 else -ACROSS)
        return pltpu.make_async_remote_copy(piece(p, c), piece(p, c), zsem.at[way, lane, src], rsem.at[p, c], device_id=(row, to), device_id_type=MESH)

    def y_copy(p, src, c):
        return pltpu.make_async_remote_copy(piece(p, c), piece(p, c), ysem.at[p, src], rsem.at[p, c], device_id=(row, mate), device_id_type=MESH)

    def w_copy(k):
        return pltpu.make_async_remote_copy(rows_w.at[row], rows_w.at[row], wsem.at[k], wrsem.at[row], device_id=(lax.rem(row + k, n_row), col), device_id_type=MESH)

    def f_copy(c):
        return pltpu.make_async_remote_copy(first_out.at[c], first_in.at[c], fsem.at[c], frsem.at[c], device_id=(pair, col), device_id_type=MESH)

    def x_copy(c, k, source):
        to = lax.rem(team + k, teams)
        return pltpu.make_async_remote_copy(chip.at[c], far_in.at[source, c], xsem.at[k, c], xrsem.at[source, c], device_id=(to * CORES + core, col), device_id_type=MESH)

    def rows_of(which):
        return pl.ds(pl.multiple_of(which * part, part), part)

    def t_copy(c, which):
        ref = tile.at[c, rows_of(which)]
        return pltpu.make_async_remote_copy(ref, ref, tsem.at[c], trsem.at[c], device_id=(pair, col), device_id_type=MESH)

    root_slot = find(order, col)
    local = lax.rem(root_slot, slots)
    root_row = root_slot // slots
    root_team = root_row // CORES

    def candidate(c, which, is_left):
        parts = []
        for s in range(slots):
            if is_left:
                parts.append(rows_l[(c - n_col) + s * (n_col // slots), rows_of(which)])
            else:
                parts.append(rows_r[s, c, rows_of(which)])
        value = parts[0]
        for s in range(1, slots):
            value = jnp.where(local == s, parts[s], value)
        return value

    def stage_one(c, is_left):
        first_out[c] = candidate(c, 1 - core, is_left)
        f_copy(c).start()

    def stage_two(c, is_left):
        mine = candidate(c, core, is_left)
        f_copy(c).wait_recv()
        chip[c] = jnp.where(root_row == row, mine, first_in[c])
        for k in range(1, teams):
            x_copy(c, k, team).start()

    def stage_three(c, is_left):
        value = chip[c]
        for k in range(1, teams):
            other = lax.rem(team + k, teams)
            x_copy(c, k, other).wait_recv()
            value = jnp.where(root_team == other, far_in[other, c], value)
        tile[c, rows_of(core)] = value
        t_copy(c, core).start()

    def sources(d, body):
        sides(z, length, d, body)

    def near(d, body):
        sources(d, lambda src, side: body(src * ACROSS + y, False))

    def lefts(d, body):
        def one(q, _):
            last = jnp.abs(z - q)
            for s in range(1, slots):
                last = jnp.maximum(last, jnp.abs(z - q - s * half))

            @pl.when(last == d)
            def _():
                for across in range(ACROSS):
                    body(n_col + q * ACROSS + across, True)

            return 0

        lax.fori_loop(0, half, one, 0)

    def far(d, body):
        sources(d, lambda src, side: body(src * ACROSS + 1 - y, False))

    def along(d, side, act):
        @pl.when((z < length - 1) & ((side == 0) | (d == 0)))
        def _():
            act(0)

        @pl.when((z > 0) & ((side == 1) | (d == 0)))
        def _():
            act(1)

    def pass_on(d, pieces):
        for p in pieces:
            def one(src, side, p=p):
                @pl.when(d > 0)
                def _():
                    y_copy(p, src, src * ACROSS + y).wait_recv()

                y_copy(p, src, src * ACROSS + y).start()
                along(d, side, lambda way: z_copy(p, src, way).start())

            sources(d, one)

    def pass_late(d):
        def both(src, side):
            @pl.when(d > 0)
            def _():
                y_copy(late, src, src * ACROSS + y).wait_recv()

            @pl.when(d == 0)
            def _():
                y_copy(late, src, src * ACROSS + y).start()

            along(d, side, lambda way: z_copy(late, src, way).start())
            y_copy(late, src, src * ACROSS + 1 - y).wait_recv()
            along(d, side, lambda way: z_copy(late, src, way, 1 - y).start())

        sources(d, both)

    def arrive(d, pieces):
        def one(src, side):
            for p in pieces:
                y_copy(p, src, src * ACROSS + 1 - y).wait_recv()

        sources(d, one)

    def w_wait():
        for k in range(1, n_row):
            w_copy(k).wait_send()
            other = lax.rem(row + k, n_row)
            ref = rows_w.at[other]
            pltpu.make_async_remote_copy(ref, ref, wsem.at[k], wrsem.at[other], device_id=(other, col), device_id_type=MESH).wait_recv()

    width = tile.shape[2]
    depth = tile.shape[1]
    per = n_col // n_row
    both_out[...] = jnp.zeros_like(both_out)

    def accumulate(t):
        def one(c, _):
            src = c // ACROSS
            when = jnp.abs(z - src) + 2

            @pl.when(when == t)
            def _():
                t_copy(c, 1 - core).wait_recv()
                start = pl.multiple_of((c % per) * depth, depth)
                others = cut_two(rows_w[c // per, pl.ds(start, depth)])
                column = cut_two(tile[c])
                for s in range(slots):
                    mine = cut_two(rows_r[s, c])
                    both_out[s, :, :width] += dot3(mine, column, ((0,), (0,)))
                    both_out[s, :, width:] += dot3(mine, others, ((0,), (0,)))

            return 0

        lax.fori_loop(0, n_col, one, 0)

    early = tuple(range(late))

    def step(t, _):
        pass_on(t, early)
        pass_late(t)
        near(t, stage_one)

        @pl.when(t == 0)
        def _():
            for k in range(1, n_row):
                w_copy(k).start()

        arrive(t - 1, early)
        lefts(t - 1, stage_one)
        far(t - 1, stage_one)
        near(t, stage_two)
        lefts(t - 1, stage_two)
        far(t - 1, stage_two)
        near(t - 1, stage_three)
        lefts(t - 2, stage_three)
        far(t - 2, stage_three)

        @pl.when(t == 2)
        def _():
            w_wait()

        accumulate(t)
        return 0

    lax.fori_loop(0, length + 2, step, 0)

    def drain(d, _):
        def one(src, side):
            for p in range(late):
                y_copy(p, src, src * ACROSS + y).wait_send()
                along(d, side, lambda way: z_copy(p, src, way).wait_send())

            @pl.when(d == 0)
            def _():
                y_copy(late, src, src * ACROSS + y).wait_send()

            along(d, side, lambda way: z_copy(late, src, way).wait_send())
            along(d, side, lambda way: z_copy(late, src, way, 1 - y).wait_send())

        sources(d, one)
        return 0

    lax.fori_loop(0, length, drain, 0)

    def finish(c, _):
        f_copy(c).wait_send()
        for k in range(1, teams):
            x_copy(c, k, team).wait_send()
        t_copy(c, core).wait_send()

        @pl.when(c >= n_col)
        def _():
            t_copy(c, 1 - core).wait_recv()

        return 0

    lax.fori_loop(0, n_col + half * ACROSS, finish, 0)


def gather(n_row, n_col, order, left, right, solved):
    slots, depth, width = right.shape
    length = n_col // ACROSS
    teams = n_row // CORES
    chunks = n_col + n_col // slots
    f32 = jnp.float32
    block = (depth, width)
    part = (depth // CORES, width)
    vmem = pl.BlockSpec(memory_space=pltpu.VMEM)
    hbm = pl.BlockSpec(memory_space=pltpu.HBM)
    dma = pltpu.SemaphoreType.DMA
    return pl.pallas_call(
        functools.partial(gather_kernel, n_row, n_col, slots),
        out_shape=(
            jax.ShapeDtypeStruct((n_col,) + left.shape, f32),
            jax.ShapeDtypeStruct((slots, width, width + solved.shape[1]), f32),
            jax.ShapeDtypeStruct((chunks,) + block, f32),
        ),
        in_specs=[pl.BlockSpec(memory_space=pltpu.SMEM), hbm, hbm, hbm],
        out_specs=(vmem, vmem, vmem),
        scratch_shapes=[
            pltpu.VMEM((slots, n_col) + block, f32),
            pltpu.VMEM((n_row,) + solved.shape, f32),
            pltpu.VMEM((chunks,) + part, f32),
            pltpu.VMEM((chunks,) + part, f32),
            pltpu.VMEM((chunks,) + part, f32),
            pltpu.VMEM((teams, chunks) + part, f32),
            dma((slots + 2,)),
            dma((slots + 2, n_col)),
            dma((2, slots + 3, length)),
            dma((slots + 2, length)),
            dma((chunks,)),
            dma((chunks,)),
            dma((teams, chunks)),
            dma((teams, chunks)),
            dma((chunks,)),
            dma((chunks,)),
            dma((n_row,)),
            dma((n_row,)),
        ],
        compiler_params=pltpu.CompilerParams(collective_id=0, has_side_effects=True, vmem_limit_bytes=55 * 1024 * 1024),
        name="gather_panel",
    )(order, left, right, solved)


def cut_two(x):
    high = x.astype(jnp.bfloat16)
    return high, (x - high.astype(jnp.float32)).astype(jnp.bfloat16)


def dot3(a, b, dims):
    (ah, al), (bh, bl) = a, b

    def dot(u, v):
        return lax.dot_general(u, v, (dims, ((), ())), preferred_element_type=jnp.float32)

    return dot(ah, bh) + (dot(ah, bl) + dot(al, bh))


def update_kernel(order, ranks, rows_l, both, tile, trailing, sides_in, trail_out, rhs_out, mid_high, mid_low):
    slots, width = both.shape[0], both.shape[1]
    slot, step = pl.program_id(0), pl.program_id(1)

    @pl.when(step == 0)
    def _():
        tile_id = order[lax.axis_index("row") * slots + slot]
        rank = ranks[tile_id]
        column_rank = ranks[lax.axis_index("col")]
        lane = lax.broadcasted_iota(jnp.int32, (1, width), 1)
        sub = lax.broadcasted_iota(jnp.int32, (width, 1), 0)
        tile_left = tile[...].reshape(-1, width)
        tile_left = cut_two(jnp.where(lane < column_rank, tile_left, 0.0))
        gram = cut_two(jnp.where(sub < rank, both[slot, :, :width], 0.0))
        middle = dot3(gram, tile_left, ((1,), (1,)))
        rows = middle.shape[1]
        mid_high[:, :rows], mid_low[:, :rows] = cut_two(middle)
        mid_high[:, rows:], mid_low[:, rows:] = cut_two(jnp.where(sub < rank, both[slot, :, width:], 0.0))

    left = cut_two(rows_l[0])
    update = dot3(left, (mid_high[...], mid_low[...]), ((1,), (0,)))
    rows = trailing.shape[1]
    trail_out[...] = trailing[...] - update[:, :rows]
    rhs_out[...] = sides_in[...] - update[:, rows:]


def update(order, ranks, rows_l, both, tile, trailing, right_sides):
    slots, width = both.shape[0], both.shape[1]
    rows, columns = trailing.shape
    others = right_sides.shape[1]
    blocks = 2
    size = rows // slots // blocks
    rows_l = rows_l.reshape(slots * blocks, size, width)
    chunks, depth = tile.shape[0], tile.shape[1]
    lefts = columns // depth
    smem = pl.BlockSpec(memory_space=pltpu.SMEM)
    vmem = pl.BlockSpec(memory_space=pltpu.VMEM)

    def place(s, i):
        return (s * blocks + i, 0)

    return pl.pallas_call(
        update_kernel,
        grid=(slots, blocks),
        out_shape=(jax.ShapeDtypeStruct(trailing.shape, jnp.float32), jax.ShapeDtypeStruct(right_sides.shape, jnp.float32)),
        in_specs=[
            smem,
            smem,
            pl.BlockSpec((1, size, width), lambda s, i: (s * blocks + i, 0, 0)),
            vmem,
            pl.BlockSpec((lefts, depth, width), lambda s, i: (chunks // lefts - 1, 0, 0)),
            pl.BlockSpec((size, columns), place),
            pl.BlockSpec((size, others), place),
        ],
        out_specs=(pl.BlockSpec((size, columns), place), pl.BlockSpec((size, others), place)),
        scratch_shapes=[pltpu.VMEM((width, columns + others), jnp.bfloat16)] * 2,
        compiler_params=pltpu.CompilerParams(vmem_limit_bytes=55 * 1024 * 1024),
        name="update_panel",
    )(order, ranks, rows_l, both, tile, trailing, right_sides)


def on_device(n_row, n_col, trailing, panel_left, panel_right, panel_solved, right_sides, tile_ranks, tile_order):
    rows_l, both, tile = gather(n_row, n_col, tile_order, panel_left, panel_right, panel_solved)
    return update(tile_order, tile_ranks, rows_l, both, tile, trailing, right_sides)


def solution(mesh):
    return jax.shard_map(
        functools.partial(on_device, mesh.shape["row"], mesh.shape["col"]),
        mesh=mesh,
        in_specs=(
            P("row", "col"),
            P(("row", "col"), None),
            P("row", "col", None),
            P("row", "col"),
            P("row", "col"),
            P(),
            P(),
        ),
        out_specs=(P("row", "col"), P("row", "col")),
        check_vma=False,
    )
```

profile of v0, /device:TPU:0, one launch (start us, length us, event | category | flops | bytes accessed | tf_op | source)
XLA Modules:
  0.0 85.6 jit_solution(9459960305942145653)
XLA Ops:
  0.6 76.7 %gather_panel.1 = (f32[8,128,384]{2,1,0:T(8,128)}, f32[2,384,512]{2,1,0:T(8,128)}, f32[12,128,384]{2,1,0:T(8,128)}) custom-call(s32[8]{0:T(128)} %order.3, f32[128,384]{1,0:T(8,128)} %left.1, f32[2,128,384]{2,1,0:T(8,128)} %right.1, f32[256,128]{1,0:T(8,128)} %solved.1), custom_call_target="tpu_custom_call" | custom-call | tf_op jit(solution)/shard_map/gather_panel/pallas_call | solution.py:316
  77.4 8.3 %update_panel.1 = (f32[1024,512]{1,0:T(8,128)}, f32[1024,128]{1,0:T(8,128)}) custom-call(s32[8]{0:T(128)} %order.3, s32[8]{0:T(128)} %ranks.1, f32[4,256,384]{2,1,0:T(8,128)} %bitcast.1, f32[2,384,512]{2,1,0:T(8,128)} %get-tuple-element.6.both, f32[12,128,384]{2,1,0:T(8,128)} %get-tuple-element.7.tile, f32[1024,512]{1,0:T(8,128)} %trailing.1, ...), custom_call_target="tpu_custom_call" | custom-call | tf_op jit(solution)/shard_map/update_panel/pallas_call | solution.py:405
where the time goes:
time: 85.8 us; the launch traced here: 85.6 us
  Pallas kernels  85 us (99%)
    pallas_call x1, Pallas kernels, gather(): pl.pallas_call(functools.partial(gather_kernel, n_row, n_col, slots), out...  76.7 us
    pallas_call x1, Pallas kernels, update(): pl.pallas_call(update_kernel, grid=(slots, blocks), out_shape=(jax.ShapeD...  8.28 us

commit v1 on v0

v1 whole, which is shorter than its diff:
```python
import functools

import jax
import jax.numpy as jnp
from jax import lax
from jax.experimental import pallas as pl
from jax.experimental.pallas import tpu as pltpu
from jax.sharding import PartitionSpec as P

MESH = pl.DeviceIdType.MESH
ACROSS = 2
CORES = 2
GATHER_VMEM = 30 * 1024 * 1024
UPDATE_VMEM = 16 * 1024 * 1024


def find(order, value):
    place = jnp.int32(0)
    for i in range(order.shape[0]):
        place = jnp.where(order[i] == value, jnp.int32(i), place)
    return place


def chain(where, root_row, root_team, candidate, tile_at, first_out, first_in, chip, far_in, fs, fr, xs, xr, ts, tr):
    row, col, team, core, teams = where
    pair = team * CORES + (1 - core)

    def f_copy(u):
        return pltpu.make_async_remote_copy(first_out.at[u], first_in.at[u], fs.at[u], fr.at[u], device_id=(pair, col), device_id_type=MESH)

    def x_copy(u, k, source):
        to = lax.rem(team + k, teams)
        return pltpu.make_async_remote_copy(chip.at[u], far_in.at[source, u], xs.at[k, u], xr.at[source, u], device_id=(to * CORES + core, col), device_id_type=MESH)

    def t_copy(u, which):
        ref = tile_at(u, which)
        return pltpu.make_async_remote_copy(ref, ref, ts.at[u], tr.at[u], device_id=(pair, col), device_id_type=MESH)

    def one(u):
        first_out[u] = candidate(u, 1 - core)
        f_copy(u).start()

    def two(u):
        mine = candidate(u, core)
        f_copy(u).wait_recv()
        chip[u] = jnp.where(root_row == row, mine, first_in[u])
        for k in range(1, teams):
            x_copy(u, k, team).start()

    def three(u):
        value = chip[u]
        for k in range(1, teams):
            other = lax.rem(team + k, teams)
            x_copy(u, k, other).wait_recv()
            value = jnp.where(root_team == other, far_in[other, u], value)
        tile_at(u, core)[...] = value
        t_copy(u, core).start()

    def ready(u):
        t_copy(u, 1 - core).wait_recv()

    def drain(u):
        f_copy(u).wait_send()
        for k in range(1, teams):
            x_copy(u, k, team).wait_send()
        t_copy(u, core).wait_send()

    return one, two, three, ready, drain


def gather_kernel(n_row, n_col, slots, order, ranks, left, right, solved, trailing, sides_in, a_high, a_low, a_rest, tile_l, trail_here, sides_here,
                  rows_l, rows_r, tile_r, rows_w, both, mid_high, mid_low, rf_out, rf_in, r_chip, r_far, lf_out, lf_in, l_chip, l_far,
                  own_sem, held_sem, rsem, zsem, ysem, wsem, wrsem, rfs, rfr, rxs, rxr, rts, rtr, lfs, lfr, lxs, lxr, lts, ltr):
    length = n_col // ACROSS
    half = length // slots
    teams = n_row // CORES
    depth, width = rows_r.shape[2], rows_r.shape[3]
    cut = left.shape[0] // 2
    early, late = slots, slots + 1
    row, col = lax.axis_index("row"), lax.axis_index("col")
    z, y = col // ACROSS, col % ACROSS
    team, core = row // CORES, row % CORES
    mate = z * ACROSS + (1 - y)
    last_up, last_down = z, length - 1 - z
    most = jnp.maximum(last_up, last_down)
    through = ((z > 0) & (z < length - 1)).astype(jnp.int32)

    barrier = pltpu.get_barrier_semaphore()

    def greet(r, c):
        pl.semaphore_signal(barrier, inc=1, device_id=(r, c), device_id_type=MESH)

    @pl.when(z > 0)
    def _():
        greet(row, col - ACROSS)

    @pl.when(z < length - 1)
    def _():
        greet(row, col + ACROSS)

    greet(row, mate)
    for k in range(1, n_row):
        greet(lax.rem(row + k, n_row), col)

    def w_rows(r):
        size = solved.shape[0]
        return rows_w.at[pl.ds(pl.multiple_of(r * size, size), size)]

    own = [pltpu.make_async_copy(right.at[s], rows_r.at[s, col], own_sem.at[s]) for s in range(slots)]
    own.append(pltpu.make_async_copy(left, rows_l.at[col], own_sem.at[slots]))
    own.append(pltpu.make_async_copy(solved, w_rows(row), own_sem.at[slots + 1]))
    for copy in own:
        copy.start()
    pl.semaphore_wait(barrier, (z > 0).astype(jnp.int32) + (z < length - 1).astype(jnp.int32) + n_row)

    def piece(p, c):
        if p == early:
            return rows_l.at[c, pl.ds(0, cut)]
        if p == late:
            return rows_l.at[c, pl.ds(cut, cut)]
        return rows_r.at[p, c]

    def mine(p):
        if p == early:
            return left.at[pl.ds(0, cut)]
        if p == late:
            return left.at[pl.ds(cut, cut)]
        return right.at[p]

    def z_copy(p, src, way, across=False, fresh=False):
        c = src * ACROSS + ((1 - y) if across else y)
        lane = late + 1 if across else p
        to = col + (ACROSS if way == 0 else -ACROSS)
        return pltpu.make_async_remote_copy(mine(p) if fresh else piece(p, c), piece(p, c), zsem.at[way, lane, src], rsem.at[p, c], device_id=(row, to), device_id_type=MESH)

    def y_copy(p, src, c, fresh=False):
        return pltpu.make_async_remote_copy(mine(p) if fresh else piece(p, c), piece(p, c), ysem.at[p, src], rsem.at[p, c], device_id=(row, mate), device_id_type=MESH)

    def w_copy(k):
        return pltpu.make_async_remote_copy(solved, w_rows(row), wsem.at[k], wrsem.at[row], device_id=(lax.rem(row + k, n_row), col), device_id_type=MESH)

    def upward(act):
        pl.when(z < length - 1)(functools.partial(act, 0))

    def downward(act):
        pl.when(z > 0)(functools.partial(act, 1))

    def along(side, act):
        (upward if side == 0 else downward)(act)

    def sources(d, body):
        for side in range(2):
            src = z - d if side == 0 else z + d
            ok = (src >= 0) if side == 0 else (src < length)
            pl.when(ok & (d > 0))(functools.partial(body, src, side))

    def near(d, body):
        @pl.when(d == 0)
        def _():
            body(col)

        sources(d, lambda src, side: body(src * ACROSS + y))

    def far(d, body):
        @pl.when(d == 0)
        def _():
            body(mate)

        sources(d, lambda src, side: body(src * ACROSS + 1 - y))

    root_slot = find(order, col)
    local = lax.rem(root_slot, slots)
    root_row = root_slot // slots
    root_team = root_row // CORES
    where = (row, col, team, core, teams)

    def pick(parts):
        value = parts[0]
        for s in range(1, slots):
            value = jnp.where(local == s, parts[s], value)
        return value

    part = depth // CORES

    def rows_of(which):
        return pl.ds(pl.multiple_of(which * part, part), part)

    def r_candidate(c, which):
        return pick([rows_r[s, c, rows_of(which)] for s in range(slots)])

    r_one, r_two, r_three, r_ready, r_drain = chain(
        where, root_row, root_team, r_candidate, lambda c, which: tile_r.at[c, rows_of(which)],
        rf_out, rf_in, r_chip, r_far, rfs, rfr, rxs, rxr, rts, rtr)

    lpart = cut // CORES

    def l_rows(u, which):
        return pl.ds(pl.multiple_of((u % 2) * cut + which * lpart, lpart), lpart)

    def l_candidate(u, which):
        return pick([rows_l[u // 2 + s * half * ACROSS, l_rows(u, which)] for s in range(slots)])

    l_one, l_two, l_three, l_ready, l_drain = chain(
        where, root_row, root_team, l_candidate, lambda u, which: tile_l.at[u // 2, l_rows(u, which)],
        lf_out, lf_in, l_chip, l_far, lfs, lfr, lxs, lxr, lts, ltr)

    def lefts(d, across, which, body):
        def one(q, _):
            last = jnp.abs(z - q)
            for s in range(1, slots):
                last = jnp.maximum(last, jnp.abs(z - q - s * half))

            @pl.when(last == d)
            def _():
                body((q * ACROSS + ((1 - y) if across else y)) * 2 + which)

            return 0

        lax.fori_loop(0, half, one, 0)

    def arrived(p, c):
        ref = piece(p, c)
        pltpu.make_async_remote_copy(ref, ref, ysem.at[p, 0], rsem.at[p, c], device_id=(row, mate), device_id_type=MESH).wait_recv()

    for s in range(slots):
        upward(lambda way: z_copy(s, z, way, fresh=True).start())
        downward(lambda way: z_copy(s, z, way, fresh=True).start())
        y_copy(s, z, col, fresh=True).start()
    y_copy(late, z, col, fresh=True).start()
    for k in range(1, n_row):
        w_copy(k).start()

    def send_left(way):
        z_copy(early, z, way, fresh=True).start()
        z_copy(late, z, way, fresh=True).start()

    @pl.when((last_up == 0) & (z < length - 1))
    def _():
        send_left(0)

    @pl.when((last_down == 0) & (z > 0))
    def _():
        send_left(1)

    both[...] = jnp.zeros_like(both)
    for copy in own:
        copy.wait()
    r_one(col)
    r_two(col)

    held = [pltpu.make_async_copy(trailing, trail_here, held_sem.at[0]), pltpu.make_async_copy(sides_in, sides_here, held_sem.at[1])]
    for copy in held:
        copy.start()

    def relay_rights(t):
        for s in range(slots):
            def one(src, side, s=s):
                arrived(s, src * ACROSS + y)
                along(side, lambda way: z_copy(s, src, way).start())
                y_copy(s, src, src * ACROSS + y).start()

            sources(t, one)

    def own_lefts(t):
        @pl.when((t == last_up) & (z < length - 1))
        def _():
            send_left(0)

        @pl.when((t == last_down) & (z > 0))
        def _():
            send_left(1)

        @pl.when(t == 2)
        def _():
            arrived(late, mate)

        @pl.when((t == jnp.maximum(last_up, 2)) & (z < length - 1))
        def _():
            z_copy(late, z, 0, True).start()

        @pl.when((t == jnp.maximum(last_down, 2)) & (z > 0))
        def _():
            z_copy(late, z, 1, True).start()

        @pl.when(t == most)
        def _():
            y_copy(early, z, col, fresh=True).start()

    def left_arrives(k, d):
        def one(src, side):
            if k == 0:
                arrived(early, src * ACROSS + y)
                y_copy(early, src, src * ACROSS + y).start()
                along(side, lambda way: z_copy(early, src, way).start())
            elif k == 1:
                arrived(late, src * ACROSS + y)
                along(side, lambda way: z_copy(late, src, way).start())
            elif k == 2:
                arrived(late, src * ACROSS + 1 - y)
                along(side, lambda way: z_copy(late, src, way, True).start())
            else:
                arrived(early, src * ACROSS + 1 - y)

        if k == 3:
            @pl.when(d == 1)
            def _():
                arrived(early, mate)

        sources(d, one)

    def left_unit(k, d, body):
        lefts(d, k >= 2, 1 if k in (1, 2) else 0, body)

    def w_wait():
        for k in range(1, n_row):
            w_copy(k).wait_send()
            other = lax.rem(row + k, n_row)
            ref = w_rows(other)
            pltpu.make_async_remote_copy(ref, ref, wsem.at[k], wrsem.at[other], device_id=(other, col), device_id_type=MESH).wait_recv()

    def accumulate(d):
        def one(src, _):
            @pl.when(jnp.abs(z - src) == d)
            def _():
                for across in range(ACROSS):
                    r_ready(src * ACROSS + across)
                start = pl.multiple_of(src * (ACROSS * depth), ACROSS * depth)
                column = tile_r[pl.ds(src * ACROSS, ACROSS)].reshape(ACROSS * depth, width)
                column = cut_two(jnp.concatenate([column, rows_w[pl.ds(start, ACROSS * depth)]], axis=1))
                for s in range(slots):
                    rows = cut_two(rows_r[s, pl.ds(src * ACROSS, ACROSS)].reshape(ACROSS * depth, width))
                    both[s] += dot3(rows, column, ((0,), (0,)))

            return 0

        lax.fori_loop(0, length, one, 0)

    def step(t, _):
        d, f = t - most + through, t - most - 1
        relay_rights(t)
        own_lefts(t)
        near(t, r_one)
        left_arrives(0, d)
        left_unit(0, d, l_one)
        near(t - 1, r_three)
        far(t - 2, r_three)
        left_unit(0, d, l_two)
        left_arrives(1, d)
        left_unit(1, d, l_one)

        @pl.when(t == 1)
        def _():
            for s in range(slots):
                arrived(s, mate)

        def one(src, side):
            for s in range(slots):
                arrived(s, src * ACROSS + 1 - y)

        sources(t - 1, one)
        far(t - 1, r_one)
        near(t, r_two)
        left_arrives(3, f)
        left_unit(3, f, l_one)
        far(t - 1, r_two)
        left_unit(1, d, l_two)
        left_unit(3, f, l_two)

        @pl.when(t == 2)
        def _():
            w_wait()

        accumulate(t - 3)
        left_arrives(2, d)
        left_unit(2, d, l_one)
        left_unit(0, d - 1, l_three)
        left_unit(1, d - 1, l_three)
        left_unit(2, d - 1, l_three)
        left_unit(3, f - 1, l_three)
        left_unit(2, d, l_two)
        return 0

    lax.fori_loop(1, 2 * most + 2, step, 0)

    lane = lax.broadcasted_iota(jnp.int32, (width, mid_high.shape[2]), 1)
    sub = lax.broadcasted_iota(jnp.int32, (width, mid_high.shape[2]), 0)
    column_rank = ranks[col]

    def middle(s, _):
        rank = ranks[order[row * slots + s]]
        kept = (sub < rank) & ((lane < column_rank) | (lane >= width))
        mid_high[s], mid_low[s] = cut_two(jnp.where(kept, both[s], 0.0))
        return 0

    lax.fori_loop(0, slots, middle, 0)
    group = n_col // (slots * 2)
    size = group * left.shape[0]

    def rows(b, _):
        here = rows_l[pl.ds(b * group, group)].reshape(size, width)
        s = b // 2
        value = dot3(cut_two(here), (mid_high[s], mid_low[s]), ((1,), (0,)))
        place = pl.ds(pl.multiple_of(b * size, size), size)
        a_high[place], a_low[place] = cut_two(value[:, :width])
        a_rest[place] = value[:, width:]
        return 0

    lax.fori_loop(0, slots * 2, rows, 0)
    left_unit(3, most, l_three)

    def drain(d, _):
        def one(src, side):
            for p in range(late):
                y_copy(p, src, src * ACROSS + y).wait_send()
            for p in range(late + 1):
                along(side, lambda way: z_copy(p, src, way).wait_send())
            along(side, lambda way: z_copy(late, src, way, True).wait_send())

        sources(d, one)
        return 0

    for p in range(late + 1):
        y_copy(p, z, col).wait_send()
        upward(lambda way: z_copy(p, z, way).wait_send())
        downward(lambda way: z_copy(p, z, way).wait_send())
    upward(lambda way: z_copy(late, z, way, True).wait_send())
    downward(lambda way: z_copy(late, z, way, True).wait_send())
    lax.fori_loop(1, length, drain, 0)

    def finish(u, _):
        r_drain(u)
        return 0

    lax.fori_loop(0, n_col, finish, 0)
    for copy in held:
        copy.wait()

    def finish_left(u, _):
        l_drain(u)
        l_ready(u)
        return 0

    lax.fori_loop(0, tile_l.shape[0] * 2, finish_left, 0)


def gather(n_row, n_col, order, ranks, left, right, solved, trailing, sides_in):
    slots, depth, width = right.shape
    length = n_col // ACROSS
    teams = n_row // CORES
    f32 = jnp.float32
    lrows = left.shape[0]
    lefts = n_col // slots
    vmem = pl.BlockSpec(memory_space=pltpu.VMEM)
    hbm = pl.BlockSpec(memory_space=pltpu.HBM)
    smem = pl.BlockSpec(memory_space=pltpu.SMEM)
    dma = pltpu.SemaphoreType.DMA
    r_units, r_part = n_col, (depth // CORES, width)
    l_units, l_part = 2 * lefts, (lrows // 2 // CORES, width)

    def buffers(units, part):
        return [pltpu.VMEM((units,) + part, f32)] * 3 + [pltpu.VMEM((teams, units) + part, f32)]

    def sems(units):
        return [dma((units,)), dma((units,)), dma((teams, units)), dma((teams, units)), dma((units,)), dma((units,))]

    return pl.pallas_call(
        functools.partial(gather_kernel, n_row, n_col, slots),
        out_shape=(
            jax.ShapeDtypeStruct((n_col * lrows, width), jnp.bfloat16),
            jax.ShapeDtypeStruct((n_col * lrows, width), jnp.bfloat16),
            jax.ShapeDtypeStruct((n_col * lrows, solved.shape[1]), f32),
            jax.ShapeDtypeStruct((lefts,) + left.shape, f32),
            jax.ShapeDtypeStruct(trailing.shape, f32),
            jax.ShapeDtypeStruct(sides_in.shape, f32),
        ),
        in_specs=[smem, smem, hbm, hbm, hbm, hbm, hbm],
        out_specs=(vmem,) * 6,
        scratch_shapes=[
            pltpu.VMEM((n_col,) + left.shape, f32),
            pltpu.VMEM((slots, n_col, depth, width), f32),
            pltpu.VMEM((n_col, depth, width), f32),
            pltpu.VMEM((n_row * solved.shape[0], solved.shape[1]), f32),
            pltpu.VMEM((slots, width, width + solved.shape[1]), f32),
            pltpu.VMEM((slots, width, width + solved.shape[1]), jnp.bfloat16),
            pltpu.VMEM((slots, width, width + solved.shape[1]), jnp.bfloat16),
            *buffers(r_units, r_part),
            *buffers(l_units, l_part),
            dma((slots + 2,)),
            dma((2,)),
            dma((slots + 2, n_col)),
            dma((2, slots + 3, length)),
            dma((slots + 2, length)),
            dma((n_row,)),
            dma((n_row,)),
            *sems(r_units),
            *sems(l_units),
        ],
        compiler_params=pltpu.CompilerParams(collective_id=0, has_side_effects=True, vmem_limit_bytes=GATHER_VMEM),
        name="gather_panel",
    )(*(pltpu.with_memory_space_constraint(a, pltpu.HBM) for a in (order, ranks, left, right, solved, trailing, sides_in)))


def cut_two(x):
    high = x.astype(jnp.bfloat16)
    return high, (x - high.astype(jnp.float32)).astype(jnp.bfloat16)


def dot3(a, b, dims):
    (ah, al), (bh, bl) = a, b

    def dot(u, v):
        return lax.dot_general(u, v, (dims, ((), ())), preferred_element_type=jnp.float32)

    return dot(ah, bh) + (dot(ah, bl) + dot(al, bh))


def update_kernel(a_high, a_low, a_rest, tile, trailing, sides_in, trail_out, rhs_out, tile_high, tile_low):
    @pl.when(pl.program_id(0) == 0)
    def _():
        tile_high[...], tile_low[...] = cut_two(tile[...].reshape(tile_high.shape))

    change = dot3((a_high[...], a_low[...]), (tile_high[...], tile_low[...]), ((1,), (1,)))
    trail_out[...] = trailing[...] - change
    rhs_out[...] = sides_in[...] - a_rest[...]


def update(a_high, a_low, a_rest, tile, trailing, right_sides):
    rows, columns = trailing.shape
    width, others = a_high.shape[1], right_sides.shape[1]
    blocks = 4
    size = rows // blocks

    def block(wide):
        return pl.BlockSpec((size, wide), lambda i: (i, 0))

    return pl.pallas_call(
        update_kernel,
        grid=(blocks,),
        out_shape=(jax.ShapeDtypeStruct(trailing.shape, jnp.float32), jax.ShapeDtypeStruct(right_sides.shape, jnp.float32)),
        in_specs=[block(width), block(width), block(others), pl.BlockSpec(tile.shape, lambda i: (0, 0, 0)), block(columns), block(others)],
        out_specs=(block(columns), block(others)),
        scratch_shapes=[pltpu.VMEM((columns, width), jnp.bfloat16)] * 2,
        compiler_params=pltpu.CompilerParams(vmem_limit_bytes=UPDATE_VMEM),
        name="update_panel",
    )(a_high, a_low, a_rest, tile, trailing, right_sides)


def on_device(n_row, n_col, trailing, panel_left, panel_right, panel_solved, right_sides, tile_ranks, tile_order):
    parts = gather(n_row, n_col, tile_order, tile_ranks, panel_left, panel_right, panel_solved, trailing, right_sides)
    return update(*parts)


def solution(mesh):
    return jax.shard_map(
        functools.partial(on_device, mesh.shape["row"], mesh.shape["col"]),
        mesh=mesh,
        in_specs=(
            P("row", "col"),
            P(("row", "col"), None),
            P("row", "col", None),
            P("row", "col"),
            P("row", "col"),
            P(),
            P(),
        ),
        out_specs=(P("row", "col"), P("row", "col")),
        check_vma=False,
    )
```

time: 85.8 us -> 68.1 us (0.79)
  Pallas kernels: 85 us -> 67.3 us
    pallas_call x1, Pallas kernels: 76.7 us -> 63.7 us  [gather(): pl.pallas_call(functools.partial(gather_kernel, n_row, n_col, slots), out...]
    pallas_call x1, Pallas kernels: 8.28 us -> 3.57 us  [update(): pl.pallas_call(update_kernel, grid=(blocks,), out_shape=(jax.ShapeDtypeSt...]
where the time goes in v1:
time: 68.1 us; the launch traced here: 67.9 us
  Pallas kernels  67.3 us (99%)
    pallas_call x1, Pallas kernels, gather(): pl.pallas_call(functools.partial(gather_kernel, n_row, n_col, slots), out...  63.7 us
    pallas_call x1, Pallas kernels, update(): pl.pallas_call(update_kernel, grid=(blocks,), out_shape=(jax.ShapeDtypeSt...  3.57 us

profile of v1, /device:TPU:0, one launch (start us, length us, event | category | flops | bytes accessed | tf_op | source)
XLA Modules:
  0.0 67.9 jit_solution(650581350559008607)
XLA Ops:
  0.6 63.7 %gather_panel.1 = (bf16[1024,384]{1,0:T(8,128)(2,1)S(1)}, bf16[1024,384]{1,0:T(8,128)(2,1)S(1)}, f32[1024,128]{1,0:T(8,128)S(1)}, f32[4,128,384]{2,1,0:T(8,128)S...) custom-call(s32[8]{0:T(128)} %order.1, s32[8]{0:T(128)} %ranks.1, f32[128,384]{1,0:T(8,128)} %left.1, ...), custom_call_target="tpu_custom_call" | custom-call | tf_op jit(solution)/shard_map/gather_panel/pallas_call | solution.py:466
  64.4 3.6 %update_panel.1 = (f32[1024,512]{1,0:T(8,128)}, f32[1024,128]{1,0:T(8,128)}) custom-call(bf16[1024,384]{1,0:T(8,128)(2,1)S(1)} %get-tuple-element.8.a_high, bf16[1024,384]{1,0:T(8,128)(2,1)S(1)} %get-tuple-element.9.a_low, f32[1024,128]{1,0:T(8,128)S(1)} %get-tuple-element.10.a_rest, f32[4,128,384]{2,1,0:T(8,128)S(1)} %get-tuple-element.11.tile, ...), custom_call_target="tpu_custom_call" | custom-call | tf_op jit(solution)/shard_map/update_panel/pallas_call | solution.py:536

commit v2 on v1

--- a/solution.py
+++ b/solution.py
@@ -21,20 +21,23 @@
     return place
 
 
-def chain(where, root_row, root_team, candidate, tile_at, first_out, first_in, chip, far_in, fs, fr, xs, xr, ts, tr):
+def chain(where, root_row, root_team, candidate, tile_at, first_out, first_in, chip, far_in, sends, fr, xr, tr):
     row, col, team, core, teams = where
     pair = team * CORES + (1 - core)
 
+    def to_pair(src, dst, sem):
+        return pltpu.make_async_remote_copy(src, dst, sends.at[0], sem, device_id=(pair, col), device_id_type=MESH)
+
     def f_copy(u):
-        return pltpu.make_async_remote_copy(first_out.at[u], first_in.at[u], fs.at[u], fr.at[u], device_id=(pair, col), device_id_type=MESH)
-
-    def x_copy(u, k, source):
+        return to_pair(first_out.at[u], first_in.at[u], fr.at[u])
+
+    def x_copy(u, k):
         to = lax.rem(team + k, teams)
-        return pltpu.make_async_remote_copy(chip.at[u], far_in.at[source, u], xs.at[k, u], xr.at[source, u], device_id=(to * CORES + core, col), device_id_type=MESH)
+        return pltpu.make_async_remote_copy(chip.at[u], far_in.at[k - 1, u], sends.at[k], xr.at[k - 1, u], device_id=(to * CORES + core, col), device_id_type=MESH)
 
     def t_copy(u, which):
         ref = tile_at(u, which)
-        return pltpu.make_async_remote_copy(ref, ref, ts.at[u], tr.at[u], device_id=(pair, col), device_id_type=MESH)
+        return pltpu.make_async_remote_copy(ref, ref, sends.at[teams], tr.at[u], device_id=(pair, col), device_id_type=MESH)
 
     def one(u):
         first_out[u] = candidate(u, 1 - core)
@@ -45,32 +48,29 @@
         f_copy(u).wait_recv()
         chip[u] = jnp.where(root_row == row, mine, first_in[u])
         for k in range(1, teams):
-            x_copy(u, k, team).start()
+            x_copy(u, k).start()
 
     def three(u):
         value = chip[u]
         for k in range(1, teams):
-            other = lax.rem(team + k, teams)
-            x_copy(u, k, other).wait_recv()
-            value = jnp.where(root_team == other, far_in[other, u], value)
+            x_copy(u, k).wait_recv()
+            value = jnp.where(root_team == lax.rem(team + teams - k, teams), far_in[k - 1, u], value)
         tile_at(u, core)[...] = value
         t_copy(u, core).start()
 
     def ready(u):
         t_copy(u, 1 - core).wait_recv()
 
-    def drain(u):
-        f_copy(u).wait_send()
-        for k in range(1, teams):
-            x_copy(u, k, team).wait_send()
-        t_copy(u, core).wait_send()
+    def drain():
+        for k in range(teams + 1):
+            pltpu.make_async_remote_copy(chip, chip, sends.at[k], fr.at[0], device_id=(pair, col), device_id_type=MESH).wait_send()
 
     return one, two, three, ready, drain
 
 
 def gather_kernel(n_row, n_col, slots, order, ranks, left, right, solved, trailing, sides_in, a_high, a_low, a_rest, tile_l, trail_here, sides_here,
                   rows_l, rows_r, tile_r, rows_w, both, mid_high, mid_low, rf_out, rf_in, r_chip, r_far, lf_out, lf_in, l_chip, l_far,
-                  own_sem, held_sem, rsem, zsem, ysem, wsem, wrsem, rfs, rfr, rxs, rxr, rts, rtr, lfs, lfr, lxs, lxr, lts, ltr):
+                  own_sem, held_sem, rsem, zsem, ysem, wsem, wrsem, r_sends, rfr, rxr, rtr, l_sends, lfr, lxr, ltr):
     length = n_col // ACROSS
     half = length // slots
     teams = n_row // CORES
@@ -106,9 +106,11 @@
         size = solved.shape[0]
         return rows_w.at[pl.ds(pl.multiple_of(r * size, size), size)]
 
-    own = [pltpu.make_async_copy(right.at[s], rows_r.at[s, col], own_sem.at[s]) for s in range(slots)]
-    own.append(pltpu.make_async_copy(left, rows_l.at[col], own_sem.at[slots]))
-    own.append(pltpu.make_async_copy(solved, w_rows(row), own_sem.at[slots + 1]))
+    own = [
+        pltpu.make_async_copy(right, rows_r.at[:, col], own_sem.at[0]),
+        pltpu.make_async_copy(left, rows_l.at[col], own_sem.at[1]),
+        pltpu.make_async_copy(solved, w_rows(row), own_sem.at[2]),
+    ]
     for copy in own:
         copy.start()
     pl.semaphore_wait(barrier, (z > 0).astype(jnp.int32) + (z < length - 1).astype(jnp.int32) + n_row)
@@ -129,15 +131,15 @@
 
     def z_copy(p, src, way, across=False, fresh=False):
         c = src * ACROSS + ((1 - y) if across else y)
-        lane = late + 1 if across else p
+        lane = 0 if p < slots else 1
         to = col + (ACROSS if way == 0 else -ACROSS)
-        return pltpu.make_async_remote_copy(mine(p) if fresh else piece(p, c), piece(p, c), zsem.at[way, lane, src], rsem.at[p, c], device_id=(row, to), device_id_type=MESH)
+        return pltpu.make_async_remote_copy(mine(p) if fresh else piece(p, c), piece(p, c), zsem.at[lane, way, src], rsem.at[p, c], device_id=(row, to), device_id_type=MESH)
 
     def y_copy(p, src, c, fresh=False):
-        return pltpu.make_async_remote_copy(mine(p) if fresh else piece(p, c), piece(p, c), ysem.at[p, src], rsem.at[p, c], device_id=(row, mate), device_id_type=MESH)
+        return pltpu.make_async_remote_copy(mine(p) if fresh else piece(p, c), piece(p, c), ysem.at[max(p - slots + 1, 0)], rsem.at[p, c], device_id=(row, mate), device_id_type=MESH)
 
     def w_copy(k):
-        return pltpu.make_async_remote_copy(solved, w_rows(row), wsem.at[k], wrsem.at[row], device_id=(lax.rem(row + k, n_row), col), device_id_type=MESH)
+        return pltpu.make_async_remote_copy(solved, w_rows(row), wsem.at[0], wrsem.at[0], device_id=(lax.rem(row + k, n_row), col), device_id_type=MESH)
 
     def upward(act):
         pl.when(z < length - 1)(functools.partial(act, 0))
@@ -190,7 +192,7 @@
 
     r_one, r_two, r_three, r_ready, r_drain = chain(
         where, root_row, root_team, r_candidate, lambda c, which: tile_r.at[c, rows_of(which)],
-        rf_out, rf_in, r_chip, r_far, rfs, rfr, rxs, rxr, rts, rtr)
+        rf_out, rf_in, r_chip, r_far, r_sends, rfr, rxr, rtr)
 
     lpart = cut // CORES
 
@@ -202,7 +204,7 @@
 
     l_one, l_two, l_three, l_ready, l_drain = chain(
         where, root_row, root_team, l_candidate, lambda u, which: tile_l.at[u // 2, l_rows(u, which)],
-        lf_out, lf_in, l_chip, l_far, lfs, lfr, lxs, lxr, lts, ltr)
+        lf_out, lf_in, l_chip, l_far, l_sends, lfr, lxr, ltr)
 
     def lefts(d, across, which, body):
         def one(q, _):
@@ -220,7 +222,7 @@
 
     def arrived(p, c):
         ref = piece(p, c)
-        pltpu.make_async_remote_copy(ref, ref, ysem.at[p, 0], rsem.at[p, c], device_id=(row, mate), device_id_type=MESH).wait_recv()
+        pltpu.make_async_remote_copy(ref, ref, ysem.at[0], rsem.at[p, c], device_id=(row, mate), device_id_type=MESH).wait_recv()
 
     for s in range(slots):
         upward(lambda way: z_copy(s, z, way, fresh=True).start())
@@ -301,22 +303,14 @@
             else:
                 arrived(early, src * ACROSS + 1 - y)
 
-        if k == 3:
-            @pl.when(d == 1)
-            def _():
-                arrived(early, mate)
-
         sources(d, one)
 
     def left_unit(k, d, body):
         lefts(d, k >= 2, 1 if k in (1, 2) else 0, body)
 
     def w_wait():
-        for k in range(1, n_row):
-            w_copy(k).wait_send()
-            other = lax.rem(row + k, n_row)
-            ref = w_rows(other)
-            pltpu.make_async_remote_copy(ref, ref, wsem.at[k], wrsem.at[other], device_id=(other, col), device_id_type=MESH).wait_recv()
+        ref = rows_w.at[pl.ds(0, (n_row - 1) * solved.shape[0])]
+        pltpu.make_async_remote_copy(ref, ref, wsem.at[0], wrsem.at[0], device_id=(row, mate), device_id_type=MESH).wait()
 
     def accumulate(d):
         def one(src, _):
@@ -335,18 +329,31 @@
 
         lax.fori_loop(0, length, one, 0)
 
+    first_last = jnp.minimum(most, 2)
+
     def step(t, _):
-        d, f = t - most + through, t - most - 1
+        a = jnp.where(through == 1, t - most + 1, 0)
+        b = jnp.where(through == 1, 0, t - most + 1)
+        c = t - most + through
+        e = t - most - through
         relay_rights(t)
         own_lefts(t)
         near(t, r_one)
-        left_arrives(0, d)
-        left_unit(0, d, l_one)
-        near(t - 1, r_three)
-        far(t - 2, r_three)
-        left_unit(0, d, l_two)
-        left_arrives(1, d)
-        left_unit(1, d, l_one)
+        left_arrives(0, a)
+        left_unit(0, a, l_one)
+        left_arrives(1, a)
+        left_unit(1, a, l_one)
+        left_unit(0, a, l_two)
+        left_arrives(2, c)
+        left_unit(2, c, l_one)
+        left_unit(1, a, l_two)
+        near(t, r_two)
+        left_arrives(0, b)
+        left_unit(0, b, l_one)
+        left_arrives(1, b)
+        left_unit(1, b, l_one)
+        left_unit(0, b, l_two)
+        left_unit(2, c, l_two)
 
         @pl.when(t == 1)
         def _():
@@ -359,28 +366,48 @@
 
         sources(t - 1, one)
         far(t - 1, r_one)
-        near(t, r_two)
-        left_arrives(3, f)
-        left_unit(3, f, l_one)
+        left_unit(1, b, l_two)
+
+        @pl.when(e == first_last)
+        def _():
+            arrived(early, mate)
+            left_arrives(3, 1)
+            left_unit(3, 1, l_one)
+
+        @pl.when(e > 1)
+        def _():
+            left_arrives(3, e)
+            left_unit(3, e, l_one)
+
         far(t - 1, r_two)
-        left_unit(1, d, l_two)
-        left_unit(3, f, l_two)
+
+        @pl.when(e == first_last)
+        def _():
+            left_unit(3, 1, l_two)
+
+        @pl.when(e > 1)
+        def _():
+            left_unit(3, e, l_two)
 
         @pl.when(t == 2)
         def _():
             w_wait()
 
+        near(t - 1, r_three)
+        far(t - 2, r_three)
         accumulate(t - 3)
-        left_arrives(2, d)
-        left_unit(2, d, l_one)
-        left_unit(0, d - 1, l_three)
-        left_unit(1, d - 1, l_three)
-        left_unit(2, d - 1, l_three)
-        left_unit(3, f - 1, l_three)
-        left_unit(2, d, l_two)
         return 0
 
-    lax.fori_loop(1, 2 * most + 2, step, 0)
+    lax.fori_loop(1, jnp.maximum(2 * most + 1 + through, most + 4), step, 0)
+
+    def spread(d, _):
+        for k in range(4):
+            left_unit(k, d, l_three)
+        return 0
+
+    lax.fori_loop(1, most, spread, 0)
+    left_unit(0, most, l_three)
+    left_unit(1, most, l_three)
 
     lane = lax.broadcasted_iota(jnp.int32, (width, mid_high.shape[2]), 1)
     sub = lax.broadcasted_iota(jnp.int32, (width, mid_high.shape[2]), 0)
@@ -406,41 +433,39 @@
         return 0
 
     lax.fori_loop(0, slots * 2, rows, 0)
+    left_unit(2, most, l_three)
     left_unit(3, most, l_three)
 
-    def drain(d, _):
-        def one(src, side):
-            for p in range(late):
-                y_copy(p, src, src * ACROSS + y).wait_send()
-            for p in range(late + 1):
-                along(side, lambda way: z_copy(p, src, way).wait_send())
-            along(side, lambda way: z_copy(late, src, way, True).wait_send())
-
-        sources(d, one)
+    def leave(ref, sem):
+        pltpu.make_async_remote_copy(ref, ref, sem, rsem.at[0, 0], device_id=(row, mate), device_id_type=MESH).wait_send()
+
+    def drain(src, _):
+        @pl.when((src <= z) & (z < length - 1))
+        def _():
+            leave(rows_r.at[:, 0], zsem.at[0, 0, src])
+            leave(rows_l.at[pl.ds(0, 3), pl.ds(0, cut)], zsem.at[1, 0, src])
+
+        @pl.when((src >= z) & (z > 0))
+        def _():
+            leave(rows_r.at[:, 0], zsem.at[0, 1, src])
+            leave(rows_l.at[pl.ds(0, 3), pl.ds(0, cut)], zsem.at[1, 1, src])
+
         return 0
 
-    for p in range(late + 1):
-        y_copy(p, z, col).wait_send()
-        upward(lambda way: z_copy(p, z, way).wait_send())
-        downward(lambda way: z_copy(p, z, way).wait_send())
-    upward(lambda way: z_copy(late, z, way, True).wait_send())
-    downward(lambda way: z_copy(late, z, way, True).wait_send())
-    lax.fori_loop(1, length, drain, 0)
-
-    def finish(u, _):
-        r_drain(u)
+    lax.fori_loop(0, length, drain, 0)
+    leave(rows_r.at[:, pl.ds(0, length)], ysem.at[0])
+    leave(rows_l.at[pl.ds(0, length), pl.ds(0, cut)], ysem.at[1])
+    leave(rows_l.at[0, pl.ds(0, cut)], ysem.at[2])
+    r_drain()
+    l_drain()
+
+    def finish_left(u, _):
+        l_ready(u)
         return 0
 
-    lax.fori_loop(0, n_col, finish, 0)
+    lax.fori_loop(0, tile_l.shape[0] * 2, finish_left, 0)
     for copy in held:
         copy.wait()
-
-    def finish_left(u, _):
-        l_drain(u)
-        l_ready(u)
-        return 0
-
-    lax.fori_loop(0, tile_l.shape[0] * 2, finish_left, 0)
 
 
 def gather(n_row, n_col, order, ranks, left, right, solved, trailing, sides_in):
@@ -458,10 +483,10 @@
     l_units, l_part = 2 * lefts, (lrows // 2 // CORES, width)
 
     def buffers(units, part):
-        return [pltpu.VMEM((units,) + part, f32)] * 3 + [pltpu.VMEM((teams, units) + part, f32)]
+        return [pltpu.VMEM((units,) + part, f32)] * 3 + [pltpu.VMEM((teams - 1, units) + part, f32)]
 
     def sems(units):
-        return [dma((units,)), dma((units,)), dma((teams, units)), dma((teams, units)), dma((units,)), dma((units,))]
+        return [dma((teams + 1,)), dma((units,)), dma((teams - 1, units)), dma((units,))]
 
     return pl.pallas_call(
         functools.partial(gather_kernel, n_row, n_col, slots),
@@ -485,13 +510,13 @@
             pltpu.VMEM((slots, width, width + solved.shape[1]), jnp.bfloat16),
             *buffers(r_units, r_part),
             *buffers(l_units, l_part),
-            dma((slots + 2,)),
+            dma((3,)),
             dma((2,)),
             dma((slots + 2, n_col)),
-            dma((2, slots + 3, length)),
-            dma((slots + 2, length)),
-            dma((n_row,)),
-            dma((n_row,)),
+            dma((2, 2, length)),
+            dma((3,)),
+            dma((1,)),
+            dma((1,)),
             *sems(r_units),
             *sems(l_units),
         ],

time: 68.1 us -> 64.7 us (0.950)
  Pallas kernels: 67.3 us -> 63.9 us
    pallas_call x1, Pallas kernels: 63.7 us -> 60.4 us  [gather(): pl.pallas_call(functools.partial(gather_kernel, n_row, n_col, slots), out...]
where the time goes in v2:
time: 64.7 us; the launch traced here: 64.6 us
  Pallas kernels  63.9 us (99%)
    pallas_call x1, Pallas kernels, gather(): pl.pallas_call(functools.partial(gather_kernel, n_row, n_col, slots), out...  60.4 us
    pallas_call x1, Pallas kernels, update(): pl.pallas_call(update_kernel, grid=(blocks,), out_shape=(jax.ShapeDtypeSt...  3.57 us

profile of v2, /device:TPU:0, one launch (start us, length us, event | category | flops | bytes accessed | tf_op | source)
XLA Modules:
  0.0 64.6 jit_solution(6725633860519378062)
XLA Ops:
  0.6 60.4 %gather_panel.1 = (bf16[1024,384]{1,0:T(8,128)(2,1)S(1)}, bf16[1024,384]{1,0:T(8,128)(2,1)S(1)}, f32[1024,128]{1,0:T(8,128)S(1)}, f32[4,128,384]{2,1,0:T(8,128)S...) custom-call(s32[8]{0:T(128)} %order.1, s32[8]{0:T(128)} %ranks.1, f32[128,384]{1,0:T(8,128)} %left.1, ...), custom_call_target="tpu_custom_call" | custom-call | tf_op jit(solution)/shard_map/gather_panel/pallas_call | solution.py:491
  61.0 3.6 %update_panel.1 = (f32[1024,512]{1,0:T(8,128)}, f32[1024,128]{1,0:T(8,128)}) custom-call(bf16[1024,384]{1,0:T(8,128)(2,1)S(1)} %get-tuple-element.8.a_high, bf16[1024,384]{1,0:T(8,128)(2,1)S(1)} %get-tuple-element.9.a_low, f32[1024,128]{1,0:T(8,128)S(1)} %get-tuple-element.10.a_rest, f32[4,128,384]{2,1,0:T(8,128)S(1)} %get-tuple-element.11.tile, ...), custom_call_target="tpu_custom_call" | custom-call | tf_op jit(solution)/shard_map/update_panel/pallas_call | solution.py:561

commit v3 on v2

--- a/solution.py
+++ b/solution.py
@@ -21,7 +21,7 @@
     return place
 
 
-def chain(where, root_row, root_team, candidate, tile_at, first_out, first_in, chip, far_in, sends, fr, xr, tr):
+def chain(where, root_row, root_team, candidate, tile_at, group, first_out, first_in, chip, far_in, sends, fr, xr, tr):
     row, col, team, core, teams = where
     pair = team * CORES + (1 - core)
 
@@ -37,7 +37,7 @@
 
     def t_copy(u, which):
         ref = tile_at(u, which)
-        return pltpu.make_async_remote_copy(ref, ref, sends.at[teams], tr.at[u], device_id=(pair, col), device_id_type=MESH)
+        return pltpu.make_async_remote_copy(ref, ref, sends.at[teams], tr.at[u // group], device_id=(pair, col), device_id_type=MESH)
 
     def one(u):
         first_out[u] = candidate(u, 1 - core)
@@ -58,8 +58,9 @@
         tile_at(u, core)[...] = value
         t_copy(u, core).start()
 
-    def ready(u):
-        t_copy(u, 1 - core).wait_recv()
+    def ready(g):
+        ref = chip.at[pl.ds(g * group, group)]
+        to_pair(ref, ref, tr.at[g]).wait_recv()
 
     def drain():
         for k in range(teams + 1):
@@ -68,8 +69,8 @@
     return one, two, three, ready, drain
 
 
-def gather_kernel(n_row, n_col, slots, order, ranks, left, right, solved, trailing, sides_in, a_high, a_low, a_rest, tile_l, trail_here, sides_here,
-                  rows_l, rows_r, tile_r, rows_w, both, mid_high, mid_low, rf_out, rf_in, r_chip, r_far, lf_out, lf_in, l_chip, l_far,
+def gather_kernel(n_row, n_col, slots, order, ranks, left, right, solved, trailing, sides_in, product, tile_l, trail_here, sides_here,
+                  rows_l, rows_r, tile_r, rows_w, both, mid, tile_cut, order_here, ranks_here, rf_out, rf_in, r_chip, r_far, lf_out, lf_in, l_chip, l_far,
                   own_sem, held_sem, rsem, zsem, ysem, wsem, wrsem, r_sends, rfr, rxr, rtr, l_sends, lfr, lxr, ltr):
     length = n_col // ACROSS
     half = length // slots
@@ -110,6 +111,8 @@
         pltpu.make_async_copy(right, rows_r.at[:, col], own_sem.at[0]),
         pltpu.make_async_copy(left, rows_l.at[col], own_sem.at[1]),
         pltpu.make_async_copy(solved, w_rows(row), own_sem.at[2]),
+        pltpu.make_async_copy(order, order_here, own_sem.at[3]),
+        pltpu.make_async_copy(ranks, ranks_here, own_sem.at[4]),
     ]
     for copy in own:
         copy.start()
@@ -131,9 +134,9 @@
 
     def z_copy(p, src, way, across=False, fresh=False):
         c = src * ACROSS + ((1 - y) if across else y)
-        lane = 0 if p < slots else 1
+        lane = 0 if p < slots else (2 if across else 1)
         to = col + (ACROSS if way == 0 else -ACROSS)
-        return pltpu.make_async_remote_copy(mine(p) if fresh else piece(p, c), piece(p, c), zsem.at[lane, way, src], rsem.at[p, c], device_id=(row, to), device_id_type=MESH)
+        return pltpu.make_async_remote_copy(mine(p) if fresh else piece(p, c), piece(p, c), zsem.at[way, lane], rsem.at[p, c], device_id=(row, to), device_id_type=MESH)
 
     def y_copy(p, src, c, fresh=False):
         return pltpu.make_async_remote_copy(mine(p) if fresh else piece(p, c), piece(p, c), ysem.at[max(p - slots + 1, 0)], rsem.at[p, c], device_id=(row, mate), device_id_type=MESH)
@@ -170,41 +173,7 @@
 
         sources(d, lambda src, side: body(src * ACROSS + 1 - y))
 
-    root_slot = find(order, col)
-    local = lax.rem(root_slot, slots)
-    root_row = root_slot // slots
-    root_team = root_row // CORES
     where = (row, col, team, core, teams)
-
-    def pick(parts):
-        value = parts[0]
-        for s in range(1, slots):
-            value = jnp.where(local == s, parts[s], value)
-        return value
-
-    part = depth // CORES
-
-    def rows_of(which):
-        return pl.ds(pl.multiple_of(which * part, part), part)
-
-    def r_candidate(c, which):
-        return pick([rows_r[s, c, rows_of(which)] for s in range(slots)])
-
-    r_one, r_two, r_three, r_ready, r_drain = chain(
-        where, root_row, root_team, r_candidate, lambda c, which: tile_r.at[c, rows_of(which)],
-        rf_out, rf_in, r_chip, r_far, r_sends, rfr, rxr, rtr)
-
-    lpart = cut // CORES
-
-    def l_rows(u, which):
-        return pl.ds(pl.multiple_of((u % 2) * cut + which * lpart, lpart), lpart)
-
-    def l_candidate(u, which):
-        return pick([rows_l[u // 2 + s * half * ACROSS, l_rows(u, which)] for s in range(slots)])
-
-    l_one, l_two, l_three, l_ready, l_drain = chain(
-        where, root_row, root_team, l_candidate, lambda u, which: tile_l.at[u // 2, l_rows(u, which)],
-        lf_out, lf_in, l_chip, l_far, l_sends, lfr, lxr, ltr)
 
     def lefts(d, across, which, body):
         def one(q, _):
@@ -247,6 +216,41 @@
     both[...] = jnp.zeros_like(both)
     for copy in own:
         copy.wait()
+
+    root_slot = find(order_here, col)
+    local = lax.rem(root_slot, slots)
+    root_row = root_slot // slots
+    root_team = root_row // CORES
+    def pick(parts):
+        value = parts[0]
+        for s in range(1, slots):
+            value = jnp.where(local == s, parts[s], value)
+        return value
+
+    part = depth // CORES
+
+    def rows_of(which):
+        return pl.ds(pl.multiple_of(which * part, part), part)
+
+    def r_candidate(c, which):
+        return pick([rows_r[s, c, rows_of(which)] for s in range(slots)])
+
+    r_one, r_two, r_three, r_ready, r_drain = chain(
+        where, root_row, root_team, r_candidate, lambda c, which: tile_r.at[c, rows_of(which)], ACROSS,
+        rf_out, rf_in, r_chip, r_far, r_sends, rfr, rxr, rtr)
+
+    lpart = cut // CORES
+
+    def l_rows(u, which):
+        return pl.ds(pl.multiple_of((u % 2) * cut + which * lpart, lpart), lpart)
+
+    def l_candidate(u, which):
+        return pick([rows_l[u // 2 + s * half * ACROSS, l_rows(u, which)] for s in range(slots)])
+
+    l_one, l_two, l_three, l_ready, l_drain = chain(
+        where, root_row, root_team, l_candidate, lambda u, which: tile_l.at[u // 2, l_rows(u, which)], tile_l.shape[0],
+        lf_out, lf_in, l_chip, l_far, l_sends, lfr, lxr, ltr)
+
     r_one(col)
     r_two(col)
 
@@ -316,26 +320,45 @@
         def one(src, _):
             @pl.when(jnp.abs(z - src) == d)
             def _():
-                for across in range(ACROSS):
-                    r_ready(src * ACROSS + across)
+                r_ready(src)
                 start = pl.multiple_of(src * (ACROSS * depth), ACROSS * depth)
                 column = tile_r[pl.ds(src * ACROSS, ACROSS)].reshape(ACROSS * depth, width)
-                column = cut_two(jnp.concatenate([column, rows_w[pl.ds(start, ACROSS * depth)]], axis=1))
-                for s in range(slots):
-                    rows = cut_two(rows_r[s, pl.ds(src * ACROSS, ACROSS)].reshape(ACROSS * depth, width))
-                    both[s] += dot3(rows, column, ((0,), (0,)))
+                column = cut_right(jnp.concatenate([column, rows_w[pl.ds(start, ACROSS * depth)]], axis=1), 0)
+                rows = [rows_r[s, pl.ds(src * ACROSS, ACROSS)].reshape(ACROSS * depth, width) for s in range(slots)]
+                both[...] += dot(cut_left(jnp.concatenate(rows, axis=1), 0), column, ((0,), (0,)))
 
             return 0
 
         lax.fori_loop(0, length, one, 0)
 
-    first_last = jnp.minimum(most, 2)
+    first = jnp.minimum(most, 2)
+
+    def other_early(d):
+        @pl.when(d == first)
+        def _():
+            arrived(early, mate)
+            left_arrives(3, 1)
+            left_unit(3, 1, l_one)
+
+        @pl.when(d > 1)
+        def _():
+            left_arrives(3, d)
+            left_unit(3, d, l_one)
+
+    def other_early_two(d):
+        @pl.when(d == first)
+        def _():
+            left_unit(3, 1, l_two)
+
+        @pl.when(d > 1)
+        def _():
+            left_unit(3, d, l_two)
 
     def step(t, _):
         a = jnp.where(through == 1, t - most + 1, 0)
         b = jnp.where(through == 1, 0, t - most + 1)
-        c = t - most + through
-        e = t - most - through
+        c = jnp.where(through == 1, t - most + 1, jnp.where(t < 2 * most, t - most, 0))
+        e = jnp.where(t - through < 2 * most, t - most - through, 0)
         relay_rights(t)
         own_lefts(t)
         near(t, r_one)
@@ -350,10 +373,10 @@
         near(t, r_two)
         left_arrives(0, b)
         left_unit(0, b, l_one)
+        left_unit(2, c, l_two)
+        left_unit(0, b, l_two)
         left_arrives(1, b)
         left_unit(1, b, l_one)
-        left_unit(0, b, l_two)
-        left_unit(2, c, l_two)
 
         @pl.when(t == 1)
         def _():
@@ -367,105 +390,89 @@
         sources(t - 1, one)
         far(t - 1, r_one)
         left_unit(1, b, l_two)
-
-        @pl.when(e == first_last)
-        def _():
-            arrived(early, mate)
-            left_arrives(3, 1)
-            left_unit(3, 1, l_one)
-
-        @pl.when(e > 1)
-        def _():
-            left_arrives(3, e)
-            left_unit(3, e, l_one)
-
-        far(t - 1, r_two)
-
-        @pl.when(e == first_last)
-        def _():
-            left_unit(3, 1, l_two)
-
-        @pl.when(e > 1)
-        def _():
-            left_unit(3, e, l_two)
-
-        @pl.when(t == 2)
-        def _():
-            w_wait()
-
         near(t - 1, r_three)
         far(t - 2, r_three)
-        accumulate(t - 3)
+        far(t - 1, r_two)
+        other_early(e)
+
+        @pl.when(t == 2)
+        def _():
+            w_wait()
+
+        accumulate(jnp.where(t - 2 < most, t - 2, -1))
+        other_early_two(e)
         return 0
 
-    lax.fori_loop(1, jnp.maximum(2 * most + 1 + through, most + 4), step, 0)
-
-    def spread(d, _):
-        for k in range(4):
-            left_unit(k, d, l_three)
+    lax.fori_loop(1, jnp.maximum(2 * most + through, most + 3), step, 0)
+    for copy in held:
+        copy.wait()
+
+    lane = lax.broadcasted_iota(jnp.int32, (width, mid.shape[2]), 1)
+    sub = lax.broadcasted_iota(jnp.int32, (width, mid.shape[2]), 0)
+    column_rank = ranks_here[col]
+
+    def middle(s, _):
+        rank = ranks_here[order_here[row * slots + s]]
+        kept = (sub < rank) & ((lane < column_rank) | (lane >= width))
+        mid[s] = cut_right(jnp.where(kept, both[pl.ds(pl.multiple_of(s * width, width), width)], 0.0), 0)
         return 0
 
-    lax.fori_loop(1, most, spread, 0)
-    left_unit(0, most, l_three)
-    left_unit(1, most, l_three)
-
-    lane = lax.broadcasted_iota(jnp.int32, (width, mid_high.shape[2]), 1)
-    sub = lax.broadcasted_iota(jnp.int32, (width, mid_high.shape[2]), 0)
-    column_rank = ranks[col]
-
-    def middle(s, _):
-        rank = ranks[order[row * slots + s]]
-        kept = (sub < rank) & ((lane < column_rank) | (lane >= width))
-        mid_high[s], mid_low[s] = cut_two(jnp.where(kept, both[s], 0.0))
+    group = n_col // slots
+    size = group * left.shape[0]
+    own_slot = z // half
+
+    def rows(i, _):
+        b = lax.rem(own_slot + i, slots)
+        here = rows_l[pl.ds(b * group, group)].reshape(size, width)
+        value = dot(cut_left(here, 1), mid[b], ((1,), (0,)))
+        place = pl.ds(pl.multiple_of(b * size, size), size)
+        product[place] = cut_left(value[:, :width], 1)
+        sides_here[place] -= value[:, width:]
         return 0
 
+    blocks = tile_l.shape[0] // 2
+    soon = (2 * z // length) * blocks
+    later = blocks - soon
+
+    def spread(u, _):
+        l_three(u)
+        return 0
+
+    final = jnp.where(through == 1, 0, most)
+    left_arrives(2, final)
+    left_unit(2, final, l_one)
+    other_early(most)
+    accumulate(most)
+    left_unit(2, final, l_two)
+    other_early_two(most)
     lax.fori_loop(0, slots, middle, 0)
-    group = n_col // (slots * 2)
-    size = group * left.shape[0]
-
-    def rows(b, _):
-        here = rows_l[pl.ds(b * group, group)].reshape(size, width)
-        s = b // 2
-        value = dot3(cut_two(here), (mid_high[s], mid_low[s]), ((1,), (0,)))
-        place = pl.ds(pl.multiple_of(b * size, size), size)
-        a_high[place], a_low[place] = cut_two(value[:, :width])
-        a_rest[place] = value[:, width:]
-        return 0
-
-    lax.fori_loop(0, slots * 2, rows, 0)
-    left_unit(2, most, l_three)
-    left_unit(3, most, l_three)
+    lax.fori_loop(0, 1, rows, 0)
+    lax.fori_loop(soon * 2, (soon + blocks) * 2, spread, 0)
+    lax.fori_loop(1, slots, rows, 0)
+    l_ready(soon // blocks)
+    wide = tile_cut.shape[0]
+    tile_cut[...] = cut_right(tile_l[pl.ds(soon, blocks)].reshape(wide, width), 1)
+    columns = pl.ds(pl.multiple_of(soon * left.shape[0], wide), wide)
+    trail_here[:, columns] -= dot(product[...], tile_cut[...], ((1,), (1,)))
+    lax.fori_loop(later * 2, (later + blocks) * 2, spread, 0)
 
     def leave(ref, sem):
         pltpu.make_async_remote_copy(ref, ref, sem, rsem.at[0, 0], device_id=(row, mate), device_id_type=MESH).wait_send()
 
-    def drain(src, _):
-        @pl.when((src <= z) & (z < length - 1))
-        def _():
-            leave(rows_r.at[:, 0], zsem.at[0, 0, src])
-            leave(rows_l.at[pl.ds(0, 3), pl.ds(0, cut)], zsem.at[1, 0, src])
-
-        @pl.when((src >= z) & (z > 0))
-        def _():
-            leave(rows_r.at[:, 0], zsem.at[0, 1, src])
-            leave(rows_l.at[pl.ds(0, 3), pl.ds(0, cut)], zsem.at[1, 1, src])
-
-        return 0
-
-    lax.fori_loop(0, length, drain, 0)
+    for count in range(1, length):
+        for way, last in ((0, last_up), (1, last_down)):
+            @pl.when(last == count - 1)
+            def _(way=way, sent=count):
+                leave(rows_r.at[:, pl.ds(0, sent)], zsem.at[way, 0])
+                leave(rows_l.at[pl.ds(0, sent)], zsem.at[way, 1])
+                leave(rows_l.at[pl.ds(0, sent), pl.ds(0, cut)], zsem.at[way, 2])
+
     leave(rows_r.at[:, pl.ds(0, length)], ysem.at[0])
     leave(rows_l.at[pl.ds(0, length), pl.ds(0, cut)], ysem.at[1])
     leave(rows_l.at[0, pl.ds(0, cut)], ysem.at[2])
     r_drain()
     l_drain()
-
-    def finish_left(u, _):
-        l_ready(u)
-        return 0
-
-    lax.fori_loop(0, tile_l.shape[0] * 2, finish_left, 0)
-    for copy in held:
-        copy.wait()
+    l_ready(later // blocks)
 
 
 def gather(n_row, n_col, order, ranks, left, right, solved, trailing, sides_in):
@@ -477,7 +484,6 @@
     lefts = n_col // slots
     vmem = pl.BlockSpec(memory_space=pltpu.VMEM)
     hbm = pl.BlockSpec(memory_space=pltpu.HBM)
-    smem = pl.BlockSpec(memory_space=pltpu.SMEM)
     dma = pltpu.SemaphoreType.DMA
     r_units, r_part = n_col, (depth // CORES, width)
     l_units, l_part = 2 * lefts, (lrows // 2 // CORES, width)
@@ -485,40 +491,40 @@
     def buffers(units, part):
         return [pltpu.VMEM((units,) + part, f32)] * 3 + [pltpu.VMEM((teams - 1, units) + part, f32)]
 
-    def sems(units):
-        return [dma((teams + 1,)), dma((units,)), dma((teams - 1, units)), dma((units,))]
+    def sems(units, group):
+        return [dma((teams + 1,)), dma((units,)), dma((teams - 1, units)), dma((units // group,))]
 
     return pl.pallas_call(
         functools.partial(gather_kernel, n_row, n_col, slots),
         out_shape=(
-            jax.ShapeDtypeStruct((n_col * lrows, width), jnp.bfloat16),
-            jax.ShapeDtypeStruct((n_col * lrows, width), jnp.bfloat16),
-            jax.ShapeDtypeStruct((n_col * lrows, solved.shape[1]), f32),
+            jax.ShapeDtypeStruct((n_col * lrows, 3 * width), jnp.bfloat16),
             jax.ShapeDtypeStruct((lefts,) + left.shape, f32),
             jax.ShapeDtypeStruct(trailing.shape, f32),
             jax.ShapeDtypeStruct(sides_in.shape, f32),
         ),
-        in_specs=[smem, smem, hbm, hbm, hbm, hbm, hbm],
-        out_specs=(vmem,) * 6,
+        in_specs=[hbm] * 7,
+        out_specs=(vmem,) * 4,
         scratch_shapes=[
             pltpu.VMEM((n_col,) + left.shape, f32),
             pltpu.VMEM((slots, n_col, depth, width), f32),
             pltpu.VMEM((n_col, depth, width), f32),
             pltpu.VMEM((n_row * solved.shape[0], solved.shape[1]), f32),
-            pltpu.VMEM((slots, width, width + solved.shape[1]), f32),
-            pltpu.VMEM((slots, width, width + solved.shape[1]), jnp.bfloat16),
-            pltpu.VMEM((slots, width, width + solved.shape[1]), jnp.bfloat16),
+            pltpu.VMEM((slots * width, width + solved.shape[1]), f32),
+            pltpu.VMEM((slots, 3 * width, width + solved.shape[1]), jnp.bfloat16),
+            pltpu.VMEM((lefts * lrows // 2, 3 * width), jnp.bfloat16),
+            pltpu.SMEM(order.shape, order.dtype),
+            pltpu.SMEM(ranks.shape, ranks.dtype),
             *buffers(r_units, r_part),
             *buffers(l_units, l_part),
-            dma((3,)),
+            dma((5,)),
             dma((2,)),
             dma((slots + 2, n_col)),
-            dma((2, 2, length)),
+            dma((2, 3)),
             dma((3,)),
             dma((1,)),
             dma((1,)),
-            *sems(r_units),
-            *sems(l_units),
+            *sems(r_units, ACROSS),
+            *sems(l_units, lefts),
         ],
         compiler_params=pltpu.CompilerParams(collective_id=0, has_side_effects=True, vmem_limit_bytes=GATHER_VMEM),
         name="gather_panel",
@@ -530,49 +536,62 @@
     return high, (x - high.astype(jnp.float32)).astype(jnp.bfloat16)
 
 
-def dot3(a, b, dims):
-    (ah, al), (bh, bl) = a, b
-
-    def dot(u, v):
-        return lax.dot_general(u, v, (dims, ((), ())), preferred_element_type=jnp.float32)
-
-    return dot(ah, bh) + (dot(ah, bl) + dot(al, bh))
-
-
-def update_kernel(a_high, a_low, a_rest, tile, trailing, sides_in, trail_out, rhs_out, tile_high, tile_low):
-    @pl.when(pl.program_id(0) == 0)
-    def _():
-        tile_high[...], tile_low[...] = cut_two(tile[...].reshape(tile_high.shape))
-
-    change = dot3((a_high[...], a_low[...]), (tile_high[...], tile_low[...]), ((1,), (1,)))
-    trail_out[...] = trailing[...] - change
-    rhs_out[...] = sides_in[...] - a_rest[...]
-
-
-def update(a_high, a_low, a_rest, tile, trailing, right_sides):
-    rows, columns = trailing.shape
-    width, others = a_high.shape[1], right_sides.shape[1]
+def cut_left(x, axis):
+    high, low = cut_two(x)
+    return jnp.concatenate([high, high, low], axis=axis)
+
+
+def cut_right(x, axis):
+    high, low = cut_two(x)
+    return jnp.concatenate([high, low, high], axis=axis)
+
+
+def dot(a, b, dims):
+    return lax.dot_general(a, b, (dims, ((), ())), preferred_element_type=jnp.float32)
+
+
+def update_kernel(length, product, tile, trailing, sides, trail_out, rhs_out, result, sems):
+    rows, wide = result.shape
     blocks = 4
     size = rows // blocks
-
-    def block(wide):
-        return pl.BlockSpec((size, wide), lambda i: (i, 0))
-
+    soon = (2 * (lax.axis_index("col") // ACROSS)) // length
+    here = pl.ds(pl.multiple_of(soon * wide, wide), wide)
+    rest = pl.ds(pl.multiple_of((1 - soon) * wide, wide), wide)
+    count = tile.shape[0] // 2
+    copies = [
+        pltpu.make_async_copy(trailing.at[:, here], trail_out.at[:, here], sems.at[0]),
+        pltpu.make_async_copy(sides, rhs_out, sems.at[1]),
+    ]
+    for copy in copies:
+        copy.start()
+    columns = cut_right(tile[pl.ds((1 - soon) * count, count)].reshape(wide, tile.shape[2]), 1)
+    for i in range(blocks):
+        place = pl.ds(i * size, size)
+        result[place] = trailing[place, rest] - dot(product[place], columns, ((1,), (1,)))
+        copies.append(pltpu.make_async_copy(result.at[place], trail_out.at[place, rest], sems.at[2 + i]))
+        copies[-1].start()
+    for copy in copies:
+        copy.wait()
+
+
+def update(n_col, product, tile, trailing, sides):
+    rows, columns = trailing.shape
+    vmem = pl.BlockSpec(memory_space=pltpu.VMEM)
+    hbm = pl.BlockSpec(memory_space=pltpu.HBM)
     return pl.pallas_call(
-        update_kernel,
-        grid=(blocks,),
-        out_shape=(jax.ShapeDtypeStruct(trailing.shape, jnp.float32), jax.ShapeDtypeStruct(right_sides.shape, jnp.float32)),
-        in_specs=[block(width), block(width), block(others), pl.BlockSpec(tile.shape, lambda i: (0, 0, 0)), block(columns), block(others)],
-        out_specs=(block(columns), block(others)),
-        scratch_shapes=[pltpu.VMEM((columns, width), jnp.bfloat16)] * 2,
+        functools.partial(update_kernel, n_col // ACROSS),
+        out_shape=(jax.ShapeDtypeStruct(trailing.shape, jnp.float32), jax.ShapeDtypeStruct(sides.shape, jnp.float32)),
+        in_specs=[vmem] * 4,
+        out_specs=(hbm, hbm),
+        scratch_shapes=[pltpu.VMEM((rows, columns // 2), jnp.float32), pltpu.SemaphoreType.DMA((6,))],
         compiler_params=pltpu.CompilerParams(vmem_limit_bytes=UPDATE_VMEM),
         name="update_panel",
-    )(a_high, a_low, a_rest, tile, trailing, right_sides)
+    )(product, tile, trailing, sides)
 
 
 def on_device(n_row, n_col, trailing, panel_left, panel_right, panel_solved, right_sides, tile_ranks, tile_order):
     parts = gather(n_row, n_col, tile_order, tile_ranks, panel_left, panel_right, panel_solved, trailing, right_sides)
-    return update(*parts)
+    return update(n_col, *parts)
 
 
 def solution(mesh):

time: 64.7 us -> 60.9 us (0.941)
  Pallas kernels: 63.9 us -> 60.1 us
    pallas_call x1, Pallas kernels: 60.4 us -> 58.3 us  [gather(): pl.pallas_call(functools.partial(gather_kernel, n_row, n_col, slots), out...]
    pallas_call x1, Pallas kernels: 3.57 us -> 1.79 us  [update(): pl.pallas_call(functools.partial(update_kernel, n_col // ACROSS), out_sha...]
where the time goes in v3:
time: 60.9 us; the launch traced here: 60.7 us
  Pallas kernels  60.1 us (99%)
  between operations  0.64 us (1%)
    pallas_call x1, Pallas kernels, gather(): pl.pallas_call(functools.partial(gather_kernel, n_row, n_col, slots), out...  58.3 us
    pallas_call x1, Pallas kernels, update(): pl.pallas_call(functools.partial(update_kernel, n_col // ACROSS), out_sha...  1.79 us

profile of v3, /device:TPU:0, one launch (start us, length us, event | category | flops | bytes accessed | tf_op | source)
XLA Modules:
  0.0 60.7 jit_solution(1209506248205080438)
XLA Ops:
  0.6 58.3 %gather_panel.1 = (bf16[1024,1152]{1,0:T(8,128)(2,1)S(1)}, f32[4,128,384]{2,1,0:T(8,128)S(1)}, f32[1024,512]{1,0:T(8,128)S(1)}, f32[1024,128]{1,0:T(8,128)S(1)}) custom-call(s32[8]{0:T(128)} %order.1, s32[8]{0:T(128)} %ranks.1, f32[128,384]{1,0:T(8,128)} %left.1, f32[2,128,384]{2,1,0:T(8,128)} %right.1, f32[256,128]{1,0:T(8,128)} %solved.1, ...), custom_call_target="tpu_custom_call" | custom-call | tf_op jit(solution)/shard_map/gather_panel/pallas_call | solution.py:497
  59.0 1.8 %update_panel.1 = (f32[1024,512]{1,0:T(8,128)}, f32[1024,128]{1,0:T(8,128)}) custom-call(bf16[1024,1152]{1,0:T(8,128)(2,1)S(1)} %get-tuple-element.6.product, f32[4,128,384]{2,1,0:T(8,128)S(1)} %get-tuple-element.7.tile, f32[1024,512]{1,0:T(8,128)S(1)} %get-tuple-element.8.trailing, f32[1024,128]{1,0:T(8,128)S(1)} %get-tuple-element.9.sides), custom_call_target="tpu_custom_call" | custom-call | tf_op jit(solution)/shard_map/update_panel/pallas_call | solution.py:581

commit v4 on v3

--- a/solution.py
+++ b/solution.py
@@ -85,6 +85,7 @@
     last_up, last_down = z, length - 1 - z
     most = jnp.maximum(last_up, last_down)
     through = ((z > 0) & (z < length - 1)).astype(jnp.int32)
+    swapped = (through == 0) & (most > 1)
 
     barrier = pltpu.get_barrier_semaphore()
 
@@ -293,10 +294,13 @@
             y_copy(early, z, col, fresh=True).start()
 
     def left_arrives(k, d):
+        def over(src, side):
+            y_copy(early, src, src * ACROSS + y).start()
+
         def one(src, side):
             if k == 0:
                 arrived(early, src * ACROSS + y)
-                y_copy(early, src, src * ACROSS + y).start()
+                pl.when(jnp.logical_not(swapped) | (d != 1))(functools.partial(over, src, side))
                 along(side, lambda way: z_copy(early, src, way).start())
             elif k == 1:
                 arrived(late, src * ACROSS + y)
@@ -308,6 +312,8 @@
                 arrived(early, src * ACROSS + 1 - y)
 
         sources(d, one)
+        if k == 0:
+            pl.when(swapped & (d == 2))(lambda: sources(1, over))
 
     def left_unit(k, d, body):
         lefts(d, k >= 2, 1 if k in (1, 2) else 0, body)
@@ -331,34 +337,24 @@
 
         lax.fori_loop(0, length, one, 0)
 
-    first = jnp.minimum(most, 2)
+
+    def open_early():
+        arrived(early, mate)
+        left_arrives(3, 1)
+        left_unit(3, 1, l_one)
 
     def other_early(d):
-        @pl.when(d == first)
-        def _():
-            arrived(early, mate)
-            left_arrives(3, 1)
-            left_unit(3, 1, l_one)
-
         @pl.when(d > 1)
         def _():
+            pl.when(d == 2)(functools.partial(arrived, early, mate))
             left_arrives(3, d)
             left_unit(3, d, l_one)
-
-    def other_early_two(d):
-        @pl.when(d == first)
-        def _():
-            left_unit(3, 1, l_two)
-
-        @pl.when(d > 1)
-        def _():
-            left_unit(3, d, l_two)
 
     def step(t, _):
         a = jnp.where(through == 1, t - most + 1, 0)
         b = jnp.where(through == 1, 0, t - most + 1)
         c = jnp.where(through == 1, t - most + 1, jnp.where(t < 2 * most, t - most, 0))
-        e = jnp.where(t - through < 2 * most, t - most - through, 0)
+        e = jnp.where((through == 0) & (t < 2 * most), t - most, 0)
         relay_rights(t)
         own_lefts(t)
         near(t, r_one)
@@ -374,7 +370,11 @@
         left_arrives(0, b)
         left_unit(0, b, l_one)
         left_unit(2, c, l_two)
+        other_early(e)
         left_unit(0, b, l_two)
+        near(t - 1, r_three)
+        far(t - 2, r_three)
+        left_unit(3, jnp.where(e > 1, e, 0), l_two)
         left_arrives(1, b)
         left_unit(1, b, l_one)
 
@@ -389,18 +389,14 @@
 
         sources(t - 1, one)
         far(t - 1, r_one)
+        far(t - 1, r_two)
         left_unit(1, b, l_two)
-        near(t - 1, r_three)
-        far(t - 2, r_three)
-        far(t - 1, r_two)
-        other_early(e)
 
         @pl.when(t == 2)
         def _():
             w_wait()
 
         accumulate(jnp.where(t - 2 < most, t - 2, -1))
-        other_early_two(e)
         return 0
 
     lax.fori_loop(1, jnp.maximum(2 * most + through, most + 3), step, 0)
@@ -439,13 +435,30 @@
         return 0
 
     final = jnp.where(through == 1, 0, most)
+    between = jnp.logical_not(swapped)
+    pl.when(between)(open_early)
     left_arrives(2, final)
     left_unit(2, final, l_one)
-    other_early(most)
     accumulate(most)
+    left_unit(3, jnp.where(between, 1, 0), l_two)
+    pl.when(swapped & (most == 2))(functools.partial(arrived, early, mate))
+    pl.when(swapped)(lambda: left_arrives(3, 1))
+
+    def rest(d, _):
+        left_arrives(3, d)
+        left_unit(3, d, l_one)
+        return 0
+
+    start = jnp.where(between, 2, most)
+    lax.fori_loop(start, most + 1, rest, 0)
+    lax.fori_loop(0, slots, middle, 0)
     left_unit(2, final, l_two)
-    other_early_two(most)
-    lax.fori_loop(0, slots, middle, 0)
+
+    def rest_two(d, _):
+        left_unit(3, d, l_two)
+        return 0
+
+    lax.fori_loop(start, most + 1, rest_two, 0)
     lax.fori_loop(0, 1, rows, 0)
     lax.fori_loop(soon * 2, (soon + blocks) * 2, spread, 0)
     lax.fori_loop(1, slots, rows, 0)

time: 60.9 us -> 60 us (0.985)
  Pallas kernels: 60.1 us -> 59.2 us
    pallas_call x1, Pallas kernels: 58.3 us -> 57.4 us  [gather(): pl.pallas_call(functools.partial(gather_kernel, n_row, n_col, slots), out...]
where the time goes in v4:
time: 60 us; the launch traced here: 59.9 us
  Pallas kernels  59.2 us (99%)
  between operations  0.64 us (1%)
    pallas_call x1, Pallas kernels, gather(): pl.pallas_call(functools.partial(gather_kernel, n_row, n_col, slots), out...  57.4 us
    pallas_call x1, Pallas kernels, update(): pl.pallas_call(functools.partial(update_kernel, n_col // ACROSS), out_sha...  1.8 us

profile of v4, /device:TPU:0, one launch (start us, length us, event | category | flops | bytes accessed | tf_op | source)
XLA Modules:
  0.0 59.9 jit_solution(18241715037536722674)
XLA Ops:
  0.6 57.4 %gather_panel.1 = (bf16[1024,1152]{1,0:T(8,128)(2,1)S(1)}, f32[4,128,384]{2,1,0:T(8,128)S(1)}, f32[1024,512]{1,0:T(8,128)S(1)}, f32[1024,128]{1,0:T(8,128)S(1)}) custom-call(s32[8]{0:T(128)} %order.1, s32[8]{0:T(128)} %ranks.1, f32[128,384]{1,0:T(8,128)} %left.1, f32[2,128,384]{2,1,0:T(8,128)} %right.1, f32[256,128]{1,0:T(8,128)} %solved.1, ...), custom_call_target="tpu_custom_call" | custom-call | tf_op jit(solution)/shard_map/gather_panel/pallas_call | solution.py:510
  58.1 1.8 %update_panel.1 = (f32[1024,512]{1,0:T(8,128)}, f32[1024,128]{1,0:T(8,128)}) custom-call(bf16[1024,1152]{1,0:T(8,128)(2,1)S(1)} %get-tuple-element.6.product, f32[4,128,384]{2,1,0:T(8,128)S(1)} %get-tuple-element.7.tile, f32[1024,512]{1,0:T(8,128)S(1)} %get-tuple-element.8.trailing, f32[1024,128]{1,0:T(8,128)S(1)} %get-tuple-element.9.sides), custom_call_target="tpu_custom_call" | custom-call | tf_op jit(solution)/shard_map/update_panel/pallas_call | solution.py:594

commit v5 on v4

--- a/solution.py
+++ b/solution.py
@@ -194,10 +194,21 @@
         ref = piece(p, c)
         pltpu.make_async_remote_copy(ref, ref, ysem.at[0], rsem.at[p, c], device_id=(row, mate), device_id_type=MESH).wait_recv()
 
+    upward_first = z + 1 > length - z
+    parts = 1
+    small = depth // parts
+
+    def begin(s, i, to, send_sem):
+        rows = pl.ds(i * small, small)
+        pltpu.make_async_remote_copy(right.at[s, rows], rows_r.at[s, col, rows], send_sem, rsem.at[s, col], device_id=(row, to), device_id_type=MESH).start()
+
     for s in range(slots):
-        upward(lambda way: z_copy(s, z, way, fresh=True).start())
-        downward(lambda way: z_copy(s, z, way, fresh=True).start())
-        y_copy(s, z, col, fresh=True).start()
+        for i in range(parts):
+            pl.when(upward_first & (z < length - 1))(functools.partial(begin, s, i, col + ACROSS, zsem.at[0, 0]))
+            pl.when(jnp.logical_not(upward_first) & (z > 0))(functools.partial(begin, s, i, col - ACROSS, zsem.at[1, 0]))
+            begin(s, i, mate, ysem.at[0])
+            pl.when(jnp.logical_not(upward_first) & (z < length - 1))(functools.partial(begin, s, i, col + ACROSS, zsem.at[0, 0]))
+            pl.when(upward_first & (z > 0))(functools.partial(begin, s, i, col - ACROSS, zsem.at[1, 0]))
     y_copy(late, z, col, fresh=True).start()
     for k in range(1, n_row):
         w_copy(k).start()

time: 60 us -> 60 us (level)
  no operation moved by 1% of the time
where the time goes in v5:
time: 60 us; the launch traced here: 59.8 us
  Pallas kernels  59.2 us (99%)
  between operations  0.64 us (1%)
    pallas_call x1, Pallas kernels, gather(): pl.pallas_call(functools.partial(gather_kernel, n_row, n_col, slots), out...  57.4 us
    pallas_call x1, Pallas kernels, update(): pl.pallas_call(functools.partial(update_kernel, n_col // ACROSS), out_sha...  1.79 us

profile of v5, /device:TPU:0, one launch (start us, length us, event | category | flops | bytes accessed | tf_op | source)
XLA Modules:
  0.0 59.8 jit_solution(12756451054108661184)
XLA Ops:
  0.6 57.4 %gather_panel.1 = (bf16[1024,1152]{1,0:T(8,128)(2,1)S(1)}, f32[4,128,384]{2,1,0:T(8,128)S(1)}, f32[1024,512]{1,0:T(8,128)S(1)}, f32[1024,128]{1,0:T(8,128)S(1)}) custom-call(s32[8]{0:T(128)} %order.1, s32[8]{0:T(128)} %ranks.1, f32[128,384]{1,0:T(8,128)} %left.1, f32[2,128,384]{2,1,0:T(8,128)} %right.1, f32[256,128]{1,0:T(8,128)} %solved.1, ...), custom_call_target="tpu_custom_call" | custom-call | tf_op jit(solution)/shard_map/gather_panel/pallas_call | solution.py:521
  58.0 1.8 %update_panel.1 = (f32[1024,512]{1,0:T(8,128)}, f32[1024,128]{1,0:T(8,128)}) custom-call(bf16[1024,1152]{1,0:T(8,128)(2,1)S(1)} %get-tuple-element.6.product, f32[4,128,384]{2,1,0:T(8,128)S(1)} %get-tuple-element.7.tile, f32[1024,512]{1,0:T(8,128)S(1)} %get-tuple-element.8.trailing, f32[1024,128]{1,0:T(8,128)S(1)} %get-tuple-element.9.sides), custom_call_target="tpu_custom_call" | custom-call | tf_op jit(solution)/shard_map/update_panel/pallas_call | solution.py:605
